TPU v7x, 32 devices: a whole 2x2x4 slice. The times are simulated.
32 devices in a mesh: dp: 8 (over z, x), ctx: 4 (over y, core).
Axes of the slice: x: 2, y: 2, z: 4, core: 2. Of those that a mesh axis runs over, the one named last changes fastest.
Arguments:
- inputs: bfloat16 [8, 512, 5376], P('dp', 'ctx'), may hold values from -6 to 6
- q_proj: bfloat16 [8, 512, 2048], P('dp', 'ctx'), may hold values from -260 to 260
- k_proj: bfloat16 [8, 512, 1024], P('dp', 'ctx'), may hold values from -260 to 260
- v_proj: bfloat16 [8, 512, 1024], P('dp', 'ctx'), may hold values from -6 to 6
- d_attn: bfloat16 [8, 512, 2048], P('dp', 'ctx'), may hold values from -6 to 6
- positions: int32 [8, 512], P('dp', 'ctx'), may hold values from 0 to 511, as said below
- windows: int32 [8], P('dp'), may hold values from 512 to 1024
- q_gain: float32 [128], replicated, may hold values from 0.7 to 5.5
- k_gain: float32 [128], replicated, may hold values from 0.7 to 5.5
- weight: bfloat16 [5376, 4096], P('dp'), may hold values from -0.078125 to 0.078125
Outputs:
- d_inputs: bfloat16 [8, 512, 5376], P('dp', 'ctx')
- d_weight_t: float32 [4096, 5376], P('ctx', 'dp')
- d_q_gain: float32 [128], replicated
- d_k_gain: float32 [128], replicated
Inputs may be any that keep to these rules, and one draw needn't show every extreme that they name: `positions`: within each sequence a position counts the tokens since its document began: it grows by one from token to token and falls to 0 where a document begins; the first token of a sequence has position 0. Some sequence holds a single document.
All inputs are finite; a program needn't handle non-finite values.
Results may differ from a plain program's by a relative error of at most 0.029.
Values may be sent and summed in bfloat16 or wider, within the bound.
A program may use at most 128 MiB of HBM per device.

v0:
```python
import math

import jax
import jax.numpy as jnp
from jax import lax
from jax.experimental import pallas as pl
from jax.experimental.pallas import tpu as pltpu
from jax.sharding import PartitionSpec as P

MESH = pl.DeviceIdType.MESH

REACH = 8


score_scale = 168.0 ** (-0.5)
rope_base = 10000.0
norm_eps = 1e-06


def from_behind(value, axis, steps):
    count = lax.axis_size(axis)
    initial, last = (max(0, -steps), min(count, count - steps))
    return lax.ppermute(value, axis, [(source, source + steps) for source in range(initial, last)])


def swapped(value, axis, bit):
    count = lax.axis_size(axis)
    return lax.ppermute(value, axis, [(source, source ^ bit) for source in range(count)])


def flipped(index, bits):
    bit = 1
    while bit <= bits:
        if bits & bit:
            index = index + bit - 2 * bit * (lax.rem(index // bit, 2))
        bit *= 2
    return index


def remote(source, target, send_sem, recv_sem, axis, index):
    return pltpu.make_async_remote_copy(
        src_ref=source,
        dst_ref=target,
        send_sem=send_sem,
        recv_sem=recv_sem,
        device_id={axis: index},
        device_id_type=MESH,
    )


def exchange_kernel(n_dp, n_ctx, reach, parts_ref, pair_ref, cols_ref, far_ref, own_sem, send_a, recv_a, send_b, recv_b):
    row = lax.axis_index("dp")
    col = lax.axis_index("ctx")
    barrier = pltpu.get_barrier_semaphore()
    for step in range(1, n_dp):
        pl.semaphore_signal(barrier, 1, device_id={"dp": lax.rem(row + step, n_dp)}, device_id_type=MESH)
    for step in range(1, n_ctx):
        pl.semaphore_signal(barrier, 1, device_id={"ctx": lax.rem(col + step, n_ctx)}, device_id_type=MESH)
    pl.semaphore_wait(barrier, n_dp + n_ctx - 2)
    for step in range(1, reach + 1):
        copy = remote(pair_ref, far_ref.at[step - 1], send_b.at[step], recv_b.at[step], "ctx", lax.rem(col + step, n_ctx))
        pl.when(col + step < n_ctx)(copy.start)
    own = pltpu.make_async_copy(parts_ref.at[row], cols_ref.at[row], own_sem)
    own.start()
    sends = []
    for step in range(1, n_dp):
        peer = lax.rem(row + step, n_dp)
        copy = remote(parts_ref.at[peer], cols_ref.at[row], send_a.at[step], recv_a.at[step], "dp", peer)
        copy.start()
        sends.append(copy)
    own.wait()
    for step in range(1, n_dp):
        source = lax.rem(row + n_dp - step, n_dp)
        remote(parts_ref.at[source], cols_ref.at[source], send_a.at[step], recv_a.at[step], "dp", source).wait_recv()
        sends[step - 1].wait_send()
    for step in range(1, reach + 1):
        copy = remote(pair_ref, far_ref.at[step - 1], send_b.at[step], recv_b.at[step], "ctx", lax.rem(col + step, n_ctx))
        pl.when(col + step < n_ctx)(copy.wait_send)
        pl.when(col >= step)(copy.wait_recv)


def exchanged(parts, pair, reach):
    n_dp, n_ctx = lax.axis_size("dp"), lax.axis_size("ctx")
    anywhere = pl.BlockSpec(memory_space=pl.ANY)
    dma = pltpu.SemaphoreType.DMA
    return pl.pallas_call(
        lambda *refs: exchange_kernel(n_dp, n_ctx, reach, *refs),
        out_shape=(
            jax.ShapeDtypeStruct(parts.shape, parts.dtype),
            jax.ShapeDtypeStruct((reach,) + pair.shape, pair.dtype),
        ),
        in_specs=[anywhere, anywhere],
        out_specs=(anywhere, anywhere),
        scratch_shapes=[dma, dma((n_dp,)), dma((n_dp,)), dma((reach + 1,)), dma((reach + 1,))],
        compiler_params=pltpu.CompilerParams(collective_id=1, has_side_effects=True),
        name="exchange",
    )(parts, pair)


def project_kernel(
    n_dp, n_ctx, d_ref, w_ref, cols_ref, back_ref, sum_ref,
    blocks, acc, outbox, terms, got, own_sem, send_g, recv_g, send_o, recv_o, send_w, recv_w,
):
    row = lax.axis_index("dp")
    col = lax.axis_index("ctx")
    line = n_dp // 2
    place = row // 2
    lane = lax.rem(row, 2)
    twin = 1 - 2 * lane
    width = w_ref.shape[1]
    bits = [1 << k for k in range(n_ctx.bit_length() - 1)]
    barrier = pltpu.get_barrier_semaphore()
    for step in range(1, n_dp):
        pl.semaphore_signal(barrier, 1, device_id={"dp": lax.rem(row + step, n_dp)}, device_id_type=MESH)
    for bit in bits:
        pl.semaphore_signal(barrier, 1, device_id={"ctx": flipped(col, bit)}, device_id_type=MESH)
    pl.semaphore_wait(barrier, n_dp - 1 + len(bits))

    def relay(block, way, target):
        return remote(blocks.at[block], blocks.at[block], send_g.at[way, block], recv_g.at[block], "dp", target)

    def arrived(block):
        relay(block, 0, lax.rem(row + 1, n_dp)).wait_recv()

    def back(block, target):
        return remote(outbox.at[block], back_ref.at[row], send_o.at[block], recv_o.at[row], "dp", target)

    def product(block):
        acc[...] = jnp.zeros_like(acc)
        depth = 1024

        @pl.loop(0, width // depth)
        def _(k):
            span = pl.ds(pl.multiple_of(k * depth, depth), depth)
            acc[...] += lax.dot_general(
                blocks[block, :, span], w_ref[:, span], (((1,), (1,)), ((), ())),
                preferred_element_type=jnp.float32,
            )

        outbox[block] = acc[...].astype(outbox.dtype)

    def answer(block):
        product(block)
        back(block, block).start()

    blocks[row] = d_ref[...]
    pl.when(place < line - 1)(lambda: relay(row, 0, row + 2).start())
    pl.when(place > 0)(lambda: relay(row, 1, row - 2).start())
    relay(row, 2, row + twin).start()
    product(row)
    own = pltpu.make_async_copy(outbox.at[row], back_ref.at[row], own_sem)
    own.start()

    @pl.loop(1, line + 1)
    def _(step):
        @pl.when(place >= step)
        def _():
            block = row - 2 * step
            arrived(block)
            pl.when(place < line - 1)(lambda: relay(block, 0, row + 2).start())
            relay(block, 2, row + twin).start()

        @pl.when(place + step < line)
        def _():
            block = row + 2 * step
            arrived(block)
            pl.when(place > 0)(lambda: relay(block, 1, row - 2).start())
            relay(block, 2, row + twin).start()

        pl.when(place >= step)(lambda: answer(row - 2 * step))
        pl.when(place + step < line)(lambda: answer(row + 2 * step))

        @pl.when(place >= step - 1)
        def _():
            block = row + twin - 2 * (step - 1)
            arrived(block)
            answer(block)

        @pl.when((step > 1) & (place + step - 1 < line))
        def _():
            block = row + twin + 2 * (step - 1)
            arrived(block)
            answer(block)

    tokens = n_dp * blocks.shape[1]
    rows = width // n_ctx
    tile = 256

    def fill(slot):
        start = flipped(col, slot) * rows

        @pl.loop(0, rows // tile)
        def _(k):
            span = pl.ds(pl.multiple_of(start + k * tile, tile), tile)
            left = blocks[:, :, span].reshape(tokens, tile)
            right = cols_ref[...].reshape(tokens, cols_ref.shape[2])
            term = lax.dot_general(
                left, right, (((0,), (0,)), ((), ())), preferred_element_type=jnp.float32
            )
            terms[slot, pl.ds(pl.multiple_of(k * tile, tile), tile), :] = term.astype(terms.dtype)

    def share(slot):
        bit = slot & -slot
        return remote(terms.at[slot], got.at[slot], send_w.at[slot], recv_w.at[slot], "ctx", flipped(col, bit))

    order = [slot for slot in range(n_ctx) if slot & 1] + [slot for slot in range(n_ctx) if not slot & 1][::-1]
    for slot in order:
        fill(slot)
        if slot & 1:
            share(slot).start()
    for bit in bits:
        for slot in reversed(range(0, n_ctx, 2 * bit)):
            share(slot + bit).wait_recv()
            if slot:
                total = terms[slot].astype(jnp.float32) + got[slot + bit].astype(jnp.float32)
                terms[slot] = total.astype(terms.dtype)
                if slot & (2 * bit):
                    share(slot).start()
            else:
                held = sum_ref[...] if bit > 1 else terms[0].astype(jnp.float32)
                sum_ref[...] = held + got[bit].astype(jnp.float32)
    for slot in range(1, n_ctx):
        share(slot).wait_send()
    own.wait()

    @pl.loop(1, n_dp)
    def _(step):
        source = lax.rem(row + step, n_dp)
        remote(outbox.at[source], back_ref.at[source], send_o.at[source], recv_o.at[source], "dp", source).wait_recv()
        back(source, source).wait_send()

    relay(row, 2, row + twin).wait_send()
    pl.when(place < line - 1)(lambda: relay(row, 0, row + 2).wait_send())
    pl.when(place > 0)(lambda: relay(row, 1, row - 2).wait_send())

    @pl.loop(1, line)
    def _(step):
        @pl.when(place >= step)
        def _():
            block = row - 2 * step
            pl.when(place < line - 1)(lambda: relay(block, 0, row + 2).wait_send())
            relay(block, 2, row + twin).wait_send()

        @pl.when(place + step < line)
        def _():
            block = row + 2 * step
            pl.when(place > 0)(lambda: relay(block, 1, row - 2).wait_send())
            relay(block, 2, row + twin).wait_send()


def projected(d_own, weight, cols):
    n_dp, n_ctx = lax.axis_size("dp"), lax.axis_size("ctx")
    toks, width = d_own.shape
    part = weight.shape[0]
    dma = pltpu.SemaphoreType.DMA
    vmem = pl.BlockSpec(memory_space=pltpu.VMEM)
    return pl.pallas_call(
        lambda *refs: project_kernel(n_dp, n_ctx, *refs),
        out_shape=(
            jax.ShapeDtypeStruct((n_dp, toks, part), jnp.bfloat16),
            jax.ShapeDtypeStruct((width // n_ctx, part), jnp.float32),
        ),
        in_specs=[vmem, vmem, vmem],
        out_specs=(pl.BlockSpec(memory_space=pl.ANY), vmem),
        scratch_shapes=[
            pltpu.VMEM((n_dp, toks, width), jnp.bfloat16),
            pltpu.VMEM((toks, part), jnp.float32),
            pltpu.VMEM((n_dp, toks, part), jnp.bfloat16),
            pltpu.VMEM((n_ctx, width // n_ctx, part), jnp.bfloat16),
            pltpu.VMEM((n_ctx, width // n_ctx, part), jnp.bfloat16),
            dma,
            dma((3, n_dp)),
            dma((n_dp,)),
            dma((n_dp,)),
            dma((n_dp,)),
            dma((n_ctx,)),
            dma((n_ctx,)),
        ],
        compiler_params=pltpu.CompilerParams(
            collective_id=2, has_side_effects=True, vmem_limit_bytes=56 * 1024 * 1024
        ),
        name="project",
    )(d_own, weight, cols)


def rotated_unit(projected_rows, gain_vector, token_pos, head_count):
    head_width = gain_vector.shape[0]
    rows_heads = projected_rows.reshape(projected_rows.shape[0], head_count, head_width)
    inverse = lax.rsqrt(jnp.mean(rows_heads * rows_heads, axis=-1, keepdims=True) + norm_eps)
    normed = rows_heads * inverse * gain_vector
    half_width = head_width // 2
    frequency = jnp.exp(
        jnp.arange(half_width, dtype=jnp.float32) * (-2.0 * math.log(rope_base) / head_width)
    )
    angles = token_pos.astype(jnp.float32)[:, None] * frequency[None, :]
    cosine_table = jnp.cos(angles)[:, None, :]
    sine_table = jnp.sin(angles)[:, None, :]
    first_half = normed[..., :half_width]
    second_half = normed[..., half_width:]
    return jnp.concatenate(
        [
            first_half * cosine_table - second_half * sine_table,
            second_half * cosine_table + first_half * sine_table,
        ],
        axis=-1,
    )


def shards(inputs, q_proj, k_proj, v_proj, d_attn, positions, windows, q_gain, k_gain, weight):
    tok_rows = inputs.shape[1]
    head_width = q_gain.shape[0]
    query_heads = q_proj.shape[2] // head_width
    key_heads = k_proj.shape[2] // head_width
    group_size = query_heads // key_heads
    token_pos = positions[0]
    window = windows[0]
    dp_count = lax.axis_size("dp")
    model_width = inputs.shape[2]
    input_parts = inputs[0].reshape(tok_rows, dp_count, model_width // dp_count).transpose(1, 0, 2)
    def query_side(projected_rows, gain_vector):
        return rotated_unit(projected_rows, gain_vector, token_pos, query_heads)

    def key_side(projected_rows, gain_vector):
        return rotated_unit(projected_rows, gain_vector, token_pos, key_heads)

    q_full, query_back = jax.vjp(query_side, q_proj[0].astype(jnp.float32), q_gain)
    k_full, key_back = jax.vjp(key_side, k_proj[0].astype(jnp.float32), k_gain)
    query_rotated = q_full.astype(jnp.bfloat16).reshape(tok_rows, key_heads, group_size, head_width)
    key_rotated = k_full.astype(jnp.bfloat16)
    v_own = v_proj[0].reshape(tok_rows, key_heads, head_width)
    reach_count = min(REACH, lax.axis_size("ctx") - 1)
    own_pair = jnp.stack([key_rotated, v_own])
    input_cols, far_pairs = exchanged(input_parts, own_pair, reach_count)
    known = jnp.arange(1, reach_count + 1) <= lax.axis_index("ctx")
    far_pairs = jnp.where(known[:, None, None, None, None], far_pairs, 0)
    all_keys = jnp.concatenate([key_rotated[None], far_pairs[:, 0]])
    all_values = jnp.concatenate([v_own[None], far_pairs[:, 1]])
    block_ids = jnp.arange(reach_count + 1, dtype=jnp.int32)
    offsets = jnp.arange(tok_rows, dtype=jnp.int32)
    distance = block_ids[None, :, None] * tok_rows + offsets[:, None, None] - offsets[None, None, :]
    allowed = (distance >= 0) & (distance < window) & (distance <= token_pos[:, None, None])
    scores = (
        jnp.einsum("ahgd,bchd->hgabc", query_rotated, all_keys, preferred_element_type=jnp.float32)
        * score_scale
    )
    scores = jnp.where(allowed, scores, -jnp.inf)
    row_max = jnp.max(scores, axis=(3, 4), keepdims=True)
    exponent = jnp.exp(scores - row_max)
    probs = exponent / jnp.sum(exponent, axis=(3, 4), keepdims=True)
    head_gradient = d_attn[0].reshape(tok_rows, key_heads, group_size, head_width)
    dprobs = jnp.einsum(
        "ahgd,bchd->hgabc", head_gradient, all_values, preferred_element_type=jnp.float32
    )
    delta = jnp.sum(probs * dprobs, axis=(3, 4), keepdims=True)
    dscores = (probs * (dprobs - delta)).astype(jnp.bfloat16)
    probs_low = probs.astype(jnp.bfloat16)
    dq_rot = (
        jnp.einsum("hgabc,bchd->ahgd", dscores, all_keys, preferred_element_type=jnp.float32)
        * score_scale
    )
    dk_blocks = (
        jnp.einsum("hgabc,ahgd->bchd", dscores, query_rotated, preferred_element_type=jnp.float32)
        * score_scale
    )
    dv_blocks = jnp.einsum(
        "hgabc,ahgd->bchd", probs_low, head_gradient, preferred_element_type=jnp.float32
    )
    dq_proj, dq_gain = query_back(dq_rot.reshape(tok_rows, query_heads, head_width))
    pair_total = jnp.stack([dk_blocks[0], dv_blocks[0]])
    for distance_steps in range(1, reach_count + 1):
        far_pair = jnp.stack([dk_blocks[distance_steps], dv_blocks[distance_steps]])
        back_pair = from_behind(far_pair.astype(jnp.bfloat16), "ctx", -distance_steps)
        pair_total = pair_total + back_pair.astype(jnp.float32)
    dk_proj, dk_gain = key_back(pair_total[0])
    dq_gain_all, dk_gain_all = lax.psum((dq_gain, dk_gain), ("dp", "ctx"))
    dv_proj = pair_total[1].reshape(tok_rows, key_heads * head_width)
    d_own = jnp.concatenate([dq_proj, dk_proj, dv_proj], axis=-1).astype(jnp.bfloat16)
    d_parts, d_weight_t = projected(d_own, weight, input_cols)
    d_inputs = d_parts.transpose(1, 0, 2).reshape(1, tok_rows, model_width)
    return (d_inputs, d_weight_t, dq_gain_all, dk_gain_all)


def solution(mesh):
    placed = (
        P("dp", "ctx", None),
        P("dp", "ctx", None),
        P("dp", "ctx", None),
        P("dp", "ctx", None),
        P("dp", "ctx", None),
        P("dp", "ctx"),
        P("dp"),
        P(),
        P(),
        P("dp", None),
    )
    return jax.shard_map(
        shards,
        mesh=mesh,
        in_specs=placed,
        out_specs=(P("dp", "ctx", None), P("ctx", "dp"), P(), P()),
        check_vma=False,
    )
```

profile of v0, /device:TPU:0, one launch (start us, length us, event | category | flops | bytes accessed | tf_op | source)
XLA Modules:
  0.0 323.5 jit_solution(7553844112866086655)
XLA Ops:
  3.8 1.8 copy.76
  5.7 1.6 copy.77
  9.0 31.8 %exchange.1 = (bf16[8,128,672]{2,1,0:T(8,128)(2,1)}, bf16[3,2,128,8,128]{4,3,2,1,0:T(8,128)(2,1)}) custom-call(bf16[8,128,672]{2,1,0:T(8,128)(2,1)} %bitcast.129, bf16[2,128,8,128]{3,2,1,0:T(8,128)(2,1)} %pad_maximum_fusion.1.refs_1_), custom_call_target="tpu_custom_call" | custom-call | tf_op jit(solution)/shard_map/exchange/pallas_call | solution.py:86
  40.8 1.6 broadcast_select_fusion
  42.5 1.2 maximum_bitcast_fusion
  48.0 2.2 reshape_squeeze.11
  50.2 2.0 copy.113
  52.3 2.2 fusion.5
  55.4 2.4 fusion.10
  57.8 1.4 fusion
  59.2 1.3 fusion.2
  60.6 1.3 copy-done
  61.9 2.4 convolution_bitcast_fusion
  64.3 2.9 copy.93
  67.2 3.3 %fusion.38 = (bf16[4,128,8,128]{3,2,1,0:T(8,128)(2,1)S(1)}, f32[4,128,8,128]{3,2,1,0:T(8,128)}) fusion(f32[8,128,4,128]{1,0,3,2:T(8,128)} %copy.93), kind=kLoop, calls=%fused_computation.90 | loop fusion | flops 1048576 | bytes 5242880 | tf_op jit(solution)/shard_map/convert.20
  70.6 1.2 copy.158
  72.8 1.3 collective-permute-start
  74.9 1.3 collective-permute-start.1
  77.1 1.3 collective-permute-start.2
  79.0 1.4 copy.130
  80.4 1.4 copy.131
  81.8 1.9 multiply_add_fusion.1
  84.7 1.2 copy.154
  88.0 2.1 fusion.19
  90.3 7.3 %collective-permute-done.1 = bf16[2,128,8,128]{3,2,1,0:T(8,128)(2,1)} collective-permute-done((bf16[2,128,8,128]{3,2,1,0:T(8,128)(2,1)}, bf16[2,128,8,128]{3,2,1,0:T(8,128)(2,1)}, u32[]{:S(2)}, u32[]{:S(2)}) %collective-permute-start.1) | collective-permute-done | bytes 524320 | tf_op jit(solution)/shard_map/ppermute | solution.py:23
  97.6 2.9 collective-permute-done.2
  100.5 1.6 fusion.21
  104.8 170.1 %project.1 = (bf16[8,128,672]{2,1,0:T(8,128)(2,1)}, f32[1024,672]{1,0:T(8,128)}) custom-call(bf16[128,4096]{1,0:T(8,128)(2,1)} %pad_maximum_fusion.refs_0_, bf16[672,4096]{1,0:T(8,128)(2,1)} %refs_1_.1, bf16[8,128,672]{2,1,0:T(8,128)(2,1)} %get-tuple-element.9.refs_2_), custom_call_target="tpu_custom_call" | custom-call | tf_op jit(solution)/shard_map/project/pallas_call | solution.py:257
  274.9 1.9 copy.99
  276.8 1.5 copy.100
  278.3 3.4 %copy.101 = f32[1024,672]{0,1:T(8,128)} copy(f32[1024,672]{1,0:T(8,128)} %get-tuple-element.25) | data formatting | bytes 5505024
  281.7 41.7 %all-reduce.4 = (f32[128]{0:T(128)}, f32[128]{0:T(128)}) all-reduce(f32[128]{0:T(128)S(1)} %get-tuple-element.28, f32[128]{0:T(128)S(1)} %get-tuple-element.30), channel_id=1, replica_groups=mesh['dp'=8,'ctx'=4] {'dp','ctx'}, use_global_device_ids=true, to_apply=%region_8.9 | all-reduce | flops 256 | bytes 2048 | tf_op jit(solution)/shard_map/psum | solution.py:375
  (81 shorter events, 18.7 us)
Async XLA Ops:
  1.7 5.6 %copy-start.11 = (f32[128]{0:T(128)S(1)}, f32[128]{0:T(128)}, u32[]{:S(2)}) copy-start(f32[128]{0:T(128)} %param.18) | copy-start | bytes 1540
  42.3 2.1 copy-start.8
  43.7 1.6 copy-start.10
  45.7 6.6 %copy-start.12 = (s32[1,128]{1,0:T(1,128)S(1)}, s32[1,128]{1,0:T(1,128)}, u32[]{:S(2)}) copy-start(s32[1,128]{1,0:T(1,128)} %param.15) | copy-start | bytes 1540
  52.3 3.1 copy-start.9
  55.4 2.4 copy-start.7
  59.2 2.7 copy-start.5
  60.6 1.3 copy-start
  67.2 3.4 %copy-start.3 = (f32[8,4,128,128]{3,2,1,0:T(8,128)S(1)}, f32[8,4,128,128]{3,2,1,0:T(8,128)}, u32[]{:S(2)}) copy-start(f32[8,4,128,128]{3,2,1,0:T(8,128)} %fusion.10) | copy-start | bytes 6291460
  70.6 7.8 %copy-start.1 = (bf16[8,2,128,4,128]{2,4,1,3,0:T(8,128)(2,1)S(1)}, bf16[8,2,128,4,128]{2,4,1,3,0:T(8,128)(2,1)}, u32[]{:S(2)}) copy-start(bf16[8,2,128,4,128]{2,4,1,3,0:T(8,128)(2,1)} %copy-done) | copy-start | bytes 6291460
  72.8 17.5 %collective-permute-start = (bf16[2,128,8,128]{3,2,1,0:T(8,128)(2,1)}, bf16[2,128,8,128]{3,2,1,0:T(8,128)(2,1)}, u32[]{:S(2)}, u32[]{:S(2)}) collective-permute-start(bf16[2,128,8,128]{3,2,1,0:T(8,128)(2,1)} %pad_maximum_fusion.2), channel_id=1, source_target_pairs={{1,0},{2,1},{3,2},{5,4},{6,5},{7,6},{9,8},{10,9},{11,10},{13,12},{... | collective-permute-start | bytes 1572872 | tf_op jit(solution)/shard_map/ppermute | solution.py:23
  74.9 22.7 %collective-permute-start.1 = (bf16[2,128,8,128]{3,2,1,0:T(8,128)(2,1)}, bf16[2,128,8,128]{3,2,1,0:T(8,128)(2,1)}, u32[]{:S(2)}, u32[]{:S(2)}) collective-permute-start(bf16[2,128,8,128]{3,2,1,0:T(8,128)(2,1)} %pad_maximum_fusion.3), channel_id=1, source_target_pairs={{2,0},{3,1},{6,4},{7,5},{10,8},{11,9},{14,12},{15,13},{18,16},{19,... | collective-permute-start | bytes 1572872 | tf_op jit(solution)/shard_map/ppermute | solution.py:23
  77.1 23.4 %collective-permute-start.2 = (bf16[2,128,8,128]{3,2,1,0:T(8,128)(2,1)}, bf16[2,128,8,128]{3,2,1,0:T(8,128)(2,1)}, u32[]{:S(2)}, u32[]{:S(2)}) collective-permute-start(bf16[2,128,8,128]{3,2,1,0:T(8,128)(2,1)} %pad_maximum_fusion.4), channel_id=1, source_target_pairs={{3,0},{7,4},{11,8},{15,12},{19,16},{23,20},{27,24},{31,28}} | collective-permute-start | bytes 1572872 | tf_op jit(solution)/shard_map/ppermute | solution.py:23
  81.8 2.9 copy-start.4
  83.7 2.2 copy-start.2
  88.0 12.5 %copy-start.6 = (f32[1,128,8,128]{3,2,1,0:T(8,128)S(1)}, f32[1,128,8,128]{3,2,1,0:T(8,128)}, u32[]{:S(2)}) copy-start(f32[1,128,8,128]{3,2,1,0:T(8,128)} %slice.78) | copy-start | bytes 1572868
where the time goes:
time: 324 us; the launch traced here: 323 us
  Pallas kernels  202 us (62%)
  blocking collectives  41.7 us (13%)
  local copies, waits for them, and re-layouts  30.1 us (9%)
  other arithmetic  25 us (8%)
  waiting for transfers between devices  10.2 us (3%)
  matrix products  8.89 us (3%)
  starting transfers between devices  3.84 us (1%)
    pallas_call x1, Pallas kernels, projected(): pl.pallas_call(lambda *refs: project_kernel(n_dp, n_ctx, *refs), out_shap...  170 us
    psum x1, blocking collectives, shards(): dq_gain_all, dk_gain_all = lax.psum((dq_gain, dk_gain), ('dp', 'ctx'))  41.7 us
    pallas_call x1, Pallas kernels, exchanged(): pl.pallas_call(lambda *refs: exchange_kernel(n_dp, n_ctx, reach, *refs),...  31.8 us
    unnamed x37, local copies, waits for them, and re-layouts  12.4 us
    ppermute x3, waiting for transfers between devices, from_behind(): lax.ppermute(value, axis, [(source, source + steps) for source in range(i...  10.2 us
  transfers between devices with their start and end apart: 3, of which 2 were waited for; matrix products, arithmetic and copies ran while one was open for 4% of the time, Pallas kernels for 0%

commit v1 on v0

--- a/solution.py
+++ b/solution.py
@@ -98,8 +98,9 @@
 
 
 def project_kernel(
-    n_dp, n_ctx, d_ref, w_ref, cols_ref, back_ref, sum_ref,
-    blocks, acc, outbox, terms, got, own_sem, send_g, recv_g, send_o, recv_o, send_w, recv_w,
+    n_dp, n_ctx, d_ref, w_ref, cols_ref, gain_ref, back_ref, sum_ref, gain_out,
+    blocks, acc, outbox, terms, got, gain_rows, gain_sent, gain_got,
+    own_sem, send_g, recv_g, send_o, recv_o, send_w, recv_w, send_r, recv_r, send_c, recv_c,
 ):
     row = lax.axis_index("dp")
     col = lax.axis_index("ctx")
@@ -147,6 +148,13 @@
     pl.when(place < line - 1)(lambda: relay(row, 0, row + 2).start())
     pl.when(place > 0)(lambda: relay(row, 1, row - 2).start())
     relay(row, 2, row + twin).start()
+
+    def gain_to(peer):
+        return remote(gain_ref, gain_rows.at[row], send_r.at[peer], recv_r.at[row], "dp", peer)
+
+    gain_rows[row] = gain_ref[...]
+    for step in range(1, n_dp):
+        gain_to(lax.rem(row + step, n_dp)).start()
     product(row)
     own = pltpu.make_async_copy(outbox.at[row], back_ref.at[row], own_sem)
     own.start()
@@ -203,22 +211,45 @@
         bit = slot & -slot
         return remote(terms.at[slot], got.at[slot], send_w.at[slot], recv_w.at[slot], "ctx", flipped(col, bit))
 
-    order = [slot for slot in range(n_ctx) if slot & 1] + [slot for slot in range(n_ctx) if not slot & 1][::-1]
-    for slot in order:
+    def merge(slot, bit):
+        share(slot + bit).wait_recv()
+        if slot:
+            total = terms[slot].astype(jnp.float32) + got[slot + bit].astype(jnp.float32)
+            terms[slot] = total.astype(terms.dtype)
+            if slot & (2 * bit):
+                share(slot).start()
+        else:
+            held = sum_ref[...] if bit > 1 else terms[0].astype(jnp.float32)
+            sum_ref[...] = held + got[bit].astype(jnp.float32)
+
+    for slot in reversed(range(0, n_ctx, 2)):
+        fill(slot + 1)
+        share(slot + 1).start()
         fill(slot)
-        if slot & 1:
-            share(slot).start()
-    for bit in bits:
+        merge(slot, 1)
+
+    for step in range(1, n_dp):
+        peer = lax.rem(row + step, n_dp)
+        remote(gain_ref, gain_rows.at[peer], send_r.at[peer], recv_r.at[peer], "dp", peer).wait_recv()
+    gain_total = gain_rows[0]
+    for peer in range(1, n_dp):
+        gain_total = gain_total + gain_rows[peer]
+    for level, bit in enumerate(bits):
+        gain_sent[level] = gain_total
+        copy = remote(
+            gain_sent.at[level], gain_got.at[level], send_c.at[level], recv_c.at[level],
+            "ctx", flipped(col, bit),
+        )
+        copy.start()
+        copy.wait()
+        gain_total = gain_total + gain_got[level]
+    gain_out[...] = gain_total
+
+    for bit in bits[1:]:
         for slot in reversed(range(0, n_ctx, 2 * bit)):
-            share(slot + bit).wait_recv()
-            if slot:
-                total = terms[slot].astype(jnp.float32) + got[slot + bit].astype(jnp.float32)
-                terms[slot] = total.astype(terms.dtype)
-                if slot & (2 * bit):
-                    share(slot).start()
-            else:
-                held = sum_ref[...] if bit > 1 else terms[0].astype(jnp.float32)
-                sum_ref[...] = held + got[bit].astype(jnp.float32)
+            merge(slot, bit)
+    for step in range(1, n_dp):
+        gain_to(lax.rem(row + step, n_dp)).wait_send()
     for slot in range(1, n_ctx):
         share(slot).wait_send()
     own.wait()
@@ -248,26 +279,31 @@
             relay(block, 2, row + twin).wait_send()
 
 
-def projected(d_own, weight, cols):
+def projected(d_own, weight, cols, gains):
     n_dp, n_ctx = lax.axis_size("dp"), lax.axis_size("ctx")
     toks, width = d_own.shape
     part = weight.shape[0]
     dma = pltpu.SemaphoreType.DMA
+    levels = n_ctx.bit_length() - 1
     vmem = pl.BlockSpec(memory_space=pltpu.VMEM)
     return pl.pallas_call(
         lambda *refs: project_kernel(n_dp, n_ctx, *refs),
         out_shape=(
             jax.ShapeDtypeStruct((n_dp, toks, part), jnp.bfloat16),
             jax.ShapeDtypeStruct((width // n_ctx, part), jnp.float32),
+            jax.ShapeDtypeStruct(gains.shape, jnp.float32),
         ),
-        in_specs=[vmem, vmem, vmem],
-        out_specs=(pl.BlockSpec(memory_space=pl.ANY), vmem),
+        in_specs=[vmem, vmem, vmem, vmem],
+        out_specs=(pl.BlockSpec(memory_space=pl.ANY), vmem, vmem),
         scratch_shapes=[
             pltpu.VMEM((n_dp, toks, width), jnp.bfloat16),
             pltpu.VMEM((toks, part), jnp.float32),
             pltpu.VMEM((n_dp, toks, part), jnp.bfloat16),
             pltpu.VMEM((n_ctx, width // n_ctx, part), jnp.bfloat16),
             pltpu.VMEM((n_ctx, width // n_ctx, part), jnp.bfloat16),
+            pltpu.VMEM((n_dp,) + gains.shape, jnp.float32),
+            pltpu.VMEM((levels,) + gains.shape, jnp.float32),
+            pltpu.VMEM((levels,) + gains.shape, jnp.float32),
             dma,
             dma((3, n_dp)),
             dma((n_dp,)),
@@ -275,12 +311,16 @@
             dma((n_dp,)),
             dma((n_ctx,)),
             dma((n_ctx,)),
+            dma((n_dp,)),
+            dma((n_dp,)),
+            dma((levels,)),
+            dma((levels,)),
         ],
         compiler_params=pltpu.CompilerParams(
             collective_id=2, has_side_effects=True, vmem_limit_bytes=56 * 1024 * 1024
         ),
         name="project",
-    )(d_own, weight, cols)
+    )(d_own, weight, cols, gains)
 
 
 def rotated_unit(projected_rows, gain_vector, token_pos, head_count):
@@ -372,10 +412,11 @@
         back_pair = from_behind(far_pair.astype(jnp.bfloat16), "ctx", -distance_steps)
         pair_total = pair_total + back_pair.astype(jnp.float32)
     dk_proj, dk_gain = key_back(pair_total[0])
-    dq_gain_all, dk_gain_all = lax.psum((dq_gain, dk_gain), ("dp", "ctx"))
     dv_proj = pair_total[1].reshape(tok_rows, key_heads * head_width)
     d_own = jnp.concatenate([dq_proj, dk_proj, dv_proj], axis=-1).astype(jnp.bfloat16)
-    d_parts, d_weight_t = projected(d_own, weight, input_cols)
+    gains = jnp.pad(jnp.stack([dq_gain, dk_gain]), ((0, 6), (0, 0)))
+    d_parts, d_weight_t, gain_sums = projected(d_own, weight, input_cols, gains)
+    dq_gain_all, dk_gain_all = gain_sums[0], gain_sums[1]
     d_inputs = d_parts.transpose(1, 0, 2).reshape(1, tok_rows, model_width)
     return (d_inputs, d_weight_t, dq_gain_all, dk_gain_all)
 

time: 324 us -> 282 us (0.87)
  blocking collectives: 41.7 us -> 0 us
  Pallas kernels: 202 us -> 198 us
    psum x1 -> x0, blocking collectives: 41.7 us -> none  [shards(): dq_gain_all, dk_gain_all = lax.psum((dq_gain, dk_gain), ('dp', 'ctx'))]
    pallas_call x1, Pallas kernels: 170 us -> 166 us  [projected(): pl.pallas_call(lambda *refs: project_kernel(n_dp, n_ctx, *refs), out_shap...]
    another operation x4 -> x5, other arithmetic: 6.47 us -> 7.24 us
  transfers between devices with their start and end apart: 3 -> 3, of which waited for: 2 -> 2; matrix products, arithmetic and copies ran while one was open for 4% -> 5% of each run, Pallas kernels for 0% -> 0%
where the time goes in v1:
time: 282 us; the launch traced here: 280 us
  Pallas kernels  198 us (70%)
  local copies, waits for them, and re-layouts  31.4 us (11%)
  other arithmetic  25.7 us (9%)
  waiting for transfers between devices  10 us (4%)
  matrix products  8.88 us (3%)
  starting transfers between devices  3.84 us (1%)
    pallas_call x1, Pallas kernels, projected(): pl.pallas_call(lambda *refs: project_kernel(n_dp, n_ctx, *refs), out_shap...  166 us
    pallas_call x1, Pallas kernels, exchanged(): pl.pallas_call(lambda *refs: exchange_kernel(n_dp, n_ctx, reach, *refs),...  31.8 us
    unnamed x37, local copies, waits for them, and re-layouts  12.4 us
    ppermute x3, waiting for transfers between devices, from_behind(): lax.ppermute(value, axis, [(source, source + steps) for source in range(i...  10 us
    another operation x4, other arithmetic  6.64 us
  transfers between devices with their start and end apart: 3, of which 2 were waited for; matrix products, arithmetic and copies ran while one was open for 5% of the time, Pallas kernels for 0%

profile of v1, /device:TPU:0, one launch (start us, length us, event | category | flops | bytes accessed | tf_op | source)
XLA Modules:
  0.0 280.0 jit_solution(975708640437271995)
XLA Ops:
  3.8 1.8 copy.76
  5.7 1.6 copy.77
  9.0 31.8 %exchange.1 = (bf16[8,128,672]{2,1,0:T(8,128)(2,1)}, bf16[3,2,128,8,128]{4,3,2,1,0:T(8,128)(2,1)}) custom-call(bf16[8,128,672]{2,1,0:T(8,128)(2,1)} %bitcast.135, bf16[2,128,8,128]{3,2,1,0:T(8,128)(2,1)} %pad_maximum_fusion.1.refs_1_), custom_call_target="tpu_custom_call" | custom-call | tf_op jit(solution)/shard_map/exchange/pallas_call | solution.py:86
  40.8 1.6 broadcast_select_fusion
  42.5 1.2 maximum_bitcast_fusion
  48.0 2.2 reshape_squeeze.11
  50.2 2.0 copy.113
  52.3 2.2 fusion.5
  55.4 2.4 fusion.10
  57.8 1.4 fusion
  59.2 1.3 fusion.2
  60.6 1.3 copy-done
  61.9 2.4 convolution_bitcast_fusion
  64.3 2.9 %copy.93 = f32[8,128,4,128]{1,0,3,2:T(8,128)} copy(f32[8,128,4,128]{3,1,2,0:T(8,128)} %convolution_bitcast_fusion) | data formatting | bytes 4194304 | tf_op jit(solution)/shard_map/hgabc,ahgd->bchd/dot_general | solution.py:402
  67.2 3.3 %fusion.38 = (bf16[4,128,8,128]{3,2,1,0:T(8,128)(2,1)S(1)}, f32[4,128,8,128]{3,2,1,0:T(8,128)}) fusion(f32[8,128,4,128]{1,0,3,2:T(8,128)} %copy.93), kind=kLoop, calls=%fused_computation.94 | loop fusion | flops 1048576 | bytes 5242880 | tf_op jit(solution)/shard_map/convert.20
  70.7 1.2 copy.158
  72.8 1.3 collective-permute-start
  74.9 1.3 collective-permute-start.1
  77.1 1.3 collective-permute-start.2
  79.0 1.4 copy.130
  80.4 1.4 copy.131
  81.8 1.9 multiply_add_fusion.1
  84.7 1.2 copy.154
  88.0 2.3 fusion.19
  90.5 7.2 %collective-permute-done.1 = bf16[2,128,8,128]{3,2,1,0:T(8,128)(2,1)} collective-permute-done((bf16[2,128,8,128]{3,2,1,0:T(8,128)(2,1)}, bf16[2,128,8,128]{3,2,1,0:T(8,128)(2,1)}, u32[]{:S(2)}, u32[]{:S(2)}) %collective-permute-start.1) | collective-permute-done | bytes 524320 | tf_op jit(solution)/shard_map/ppermute | solution.py:23
  97.6 2.9 %collective-permute-done.2 = bf16[2,128,8,128]{3,2,1,0:T(8,128)(2,1)} collective-permute-done((bf16[2,128,8,128]{3,2,1,0:T(8,128)(2,1)}, bf16[2,128,8,128]{3,2,1,0:T(8,128)(2,1)}, u32[]{:S(2)}, u32[]{:S(2)}) %collective-permute-start.2) | collective-permute-done | bytes 524320 | tf_op jit(solution)/shard_map/ppermute | solution.py:23
  100.5 1.6 fusion.21
  105.4 166.5 %project.1 = (bf16[8,128,672]{2,1,0:T(8,128)(2,1)}, f32[1024,672]{1,0:T(8,128)}, f32[8,128]{1,0:T(8,128)}) custom-call(bf16[128,4096]{1,0:T(8,128)(2,1)} %pad_maximum_fusion.refs_0_, bf16[672,4096]{1,0:T(8,128)(2,1)} %refs_1_.1, bf16[8,128,672]{2,1,0:T(8,128)(2,1)} %get-tuple-element.10.refs_2_, f32[8,128]{1,0:T(8,128)} %select_maximum_fusion.refs_3_), custom_call_target="tpu_custom_call" | custom-call | tf_op jit(solution)/shard_map/project/pallas_call | solution.py:289
  271.9 1.9 copy.99
  273.8 1.5 copy.100
  275.3 3.4 %copy.101 = f32[1024,672]{0,1:T(8,128)} copy(f32[1024,672]{1,0:T(8,128)} %get-tuple-element.27) | data formatting | bytes 5505024
  278.7 1.3 slice_bitcast_fusion.3
  (82 shorter events, 19.3 us)
Async XLA Ops:
  1.7 5.6 %copy-start.11 = (f32[128]{0:T(128)S(1)}, f32[128]{0:T(128)}, u32[]{:S(2)}) copy-start(f32[128]{0:T(128)} %param.18) | copy-start | bytes 1540
  42.3 2.1 copy-start.8
  43.7 1.6 copy-start.10
  45.7 6.6 %copy-start.12 = (s32[1,128]{1,0:T(1,128)S(1)}, s32[1,128]{1,0:T(1,128)}, u32[]{:S(2)}) copy-start(s32[1,128]{1,0:T(1,128)} %param.15) | copy-start | bytes 1540
  52.3 3.1 %copy-start.9 = (bf16[128,8,2,128,1]{0,3,2,4,1:T(8,128)(2,1)S(1)}, bf16[128,8,2,128,1]{0,3,2,4,1:T(8,128)(2,1)}, u32[]{:S(2)}) copy-start(bf16[128,8,2,128,1]{0,3,2,4,1:T(8,128)(2,1)} %copy.113) | copy-start | bytes 1572868
  55.4 2.4 copy-start.7
  59.2 2.7 copy-start.5
  60.6 1.3 copy-start
  67.2 3.4 %copy-start.3 = (f32[8,4,128,128]{3,2,1,0:T(8,128)S(1)}, f32[8,4,128,128]{3,2,1,0:T(8,128)}, u32[]{:S(2)}) copy-start(f32[8,4,128,128]{3,2,1,0:T(8,128)} %fusion.10) | copy-start | bytes 6291460
  70.6 7.8 %copy-start.1 = (bf16[8,2,128,4,128]{2,4,1,3,0:T(8,128)(2,1)S(1)}, bf16[8,2,128,4,128]{2,4,1,3,0:T(8,128)(2,1)}, u32[]{:S(2)}) copy-start(bf16[8,2,128,4,128]{2,4,1,3,0:T(8,128)(2,1)} %copy-done) | copy-start | bytes 6291460
  72.8 17.7 %collective-permute-start = (bf16[2,128,8,128]{3,2,1,0:T(8,128)(2,1)}, bf16[2,128,8,128]{3,2,1,0:T(8,128)(2,1)}, u32[]{:S(2)}, u32[]{:S(2)}) collective-permute-start(bf16[2,128,8,128]{3,2,1,0:T(8,128)(2,1)} %pad_maximum_fusion.2), channel_id=1, source_target_pairs={{1,0},{2,1},{3,2},{5,4},{6,5},{7,6},{9,8},{10,9},{11,10},{13,12},{... | collective-permute-start | bytes 1572872 | tf_op jit(solution)/shard_map/ppermute | solution.py:23
  74.9 22.7 %collective-permute-start.1 = (bf16[2,128,8,128]{3,2,1,0:T(8,128)(2,1)}, bf16[2,128,8,128]{3,2,1,0:T(8,128)(2,1)}, u32[]{:S(2)}, u32[]{:S(2)}) collective-permute-start(bf16[2,128,8,128]{3,2,1,0:T(8,128)(2,1)} %pad_maximum_fusion.3), channel_id=1, source_target_pairs={{2,0},{3,1},{6,4},{7,5},{10,8},{11,9},{14,12},{15,13},{18,16},{19,... | collective-permute-start | bytes 1572872 | tf_op jit(solution)/shard_map/ppermute | solution.py:23
  77.1 23.4 %collective-permute-start.2 = (bf16[2,128,8,128]{3,2,1,0:T(8,128)(2,1)}, bf16[2,128,8,128]{3,2,1,0:T(8,128)(2,1)}, u32[]{:S(2)}, u32[]{:S(2)}) collective-permute-start(bf16[2,128,8,128]{3,2,1,0:T(8,128)(2,1)} %pad_maximum_fusion.4), channel_id=1, source_target_pairs={{3,0},{7,4},{11,8},{15,12},{19,16},{23,20},{27,24},{31,28}} | collective-permute-start | bytes 1572872 | tf_op jit(solution)/shard_map/ppermute | solution.py:23
  81.8 2.9 %copy-start.4 = (f32[8,4,128,128]{3,2,1,0:T(8,128)S(1)}, f32[8,4,128,128]{3,2,1,0:T(8,128)}, u32[]{:S(2)}) copy-start(f32[8,4,128,128]{3,2,1,0:T(8,128)} %fusion.10) | copy-start | bytes 6291460
  83.7 2.2 copy-start.2
  88.0 12.5 %copy-start.6 = (f32[1,128,8,128]{3,2,1,0:T(8,128)S(1)}, f32[1,128,8,128]{3,2,1,0:T(8,128)}, u32[]{:S(2)}) copy-start(f32[1,128,8,128]{3,2,1,0:T(8,128)} %slice.86) | copy-start | bytes 1572868

commit v2 on v1

--- a/solution.py
+++ b/solution.py
@@ -128,7 +128,7 @@
 
     def product(block):
         acc[...] = jnp.zeros_like(acc)
-        depth = 1024
+        depth = 2048
 
         @pl.loop(0, width // depth)
         def _(k):
@@ -192,7 +192,7 @@
 
     tokens = n_dp * blocks.shape[1]
     rows = width // n_ctx
-    tile = 256
+    tile = min(512, rows)
 
     def fill(slot):
         start = flipped(col, slot) * rows

time: 282 us -> 281 us (level)
  no operation moved by 1% of the time
where the time goes in v2:
time: 281 us; the launch traced here: 279 us
  Pallas kernels  198 us (70%)
  local copies, waits for them, and re-layouts  31.4 us (11%)
  other arithmetic  25.5 us (9%)
  waiting for transfers between devices  10.2 us (4%)
  matrix products  8.88 us (3%)
  starting transfers between devices  3.84 us (1%)
    pallas_call x1, Pallas kernels, projected(): pl.pallas_call(lambda *refs: project_kernel(n_dp, n_ctx, *refs), out_shap...  166 us
    pallas_call x1, Pallas kernels, exchanged(): pl.pallas_call(lambda *refs: exchange_kernel(n_dp, n_ctx, reach, *refs),...  31.8 us
    unnamed x37, local copies, waits for them, and re-layouts  12.4 us
    ppermute x3, waiting for transfers between devices, from_behind(): lax.ppermute(value, axis, [(source, source + steps) for source in range(i...  10.2 us
    another operation x4, other arithmetic  6.47 us
  transfers between devices with their start and end apart: 3, of which 2 were waited for; matrix products, arithmetic and copies ran while one was open for 5% of the time, Pallas kernels for 0%

profile of v2, /device:TPU:0, one launch (start us, length us, event | category | flops | bytes accessed | tf_op | source)
XLA Modules:
  0.0 279.3 jit_solution(3858997533903857769)
XLA Ops:
  3.8 1.8 copy.76
  5.7 1.6 copy.77
  9.0 31.8 %exchange.1 = (bf16[8,128,672]{2,1,0:T(8,128)(2,1)}, bf16[3,2,128,8,128]{4,3,2,1,0:T(8,128)(2,1)}) custom-call(bf16[8,128,672]{2,1,0:T(8,128)(2,1)} %bitcast.135, bf16[2,128,8,128]{3,2,1,0:T(8,128)(2,1)} %pad_maximum_fusion.1.refs_1_), custom_call_target="tpu_custom_call" | custom-call | tf_op jit(solution)/shard_map/exchange/pallas_call | solution.py:86
  40.8 1.6 broadcast_select_fusion
  42.5 1.2 maximum_bitcast_fusion
  48.0 2.2 reshape_squeeze.11
  50.2 2.0 copy.113
  52.3 2.2 fusion.5
  55.4 2.4 fusion.10
  57.8 1.4 fusion
  59.2 1.3 fusion.2
  60.6 1.3 copy-done
  61.9 2.4 convolution_bitcast_fusion
  64.3 2.9 %copy.93 = f32[8,128,4,128]{1,0,3,2:T(8,128)} copy(f32[8,128,4,128]{3,1,2,0:T(8,128)} %convolution_bitcast_fusion) | data formatting | bytes 4194304 | tf_op jit(solution)/shard_map/hgabc,ahgd->bchd/dot_general | solution.py:402
  67.2 3.3 %fusion.38 = (bf16[4,128,8,128]{3,2,1,0:T(8,128)(2,1)S(1)}, f32[4,128,8,128]{3,2,1,0:T(8,128)}) fusion(f32[8,128,4,128]{1,0,3,2:T(8,128)} %copy.93), kind=kLoop, calls=%fused_computation.94 | loop fusion | flops 1048576 | bytes 5242880 | tf_op jit(solution)/shard_map/convert.20
  70.7 1.2 copy.158
  72.8 1.3 collective-permute-start
  74.9 1.3 collective-permute-start.1
  77.1 1.3 collective-permute-start.2
  79.0 1.4 copy.130
  80.4 1.4 copy.131
  81.8 1.9 multiply_add_fusion.1
  84.7 1.2 copy.154
  88.0 2.1 fusion.19
  90.3 7.3 %collective-permute-done.1 = bf16[2,128,8,128]{3,2,1,0:T(8,128)(2,1)} collective-permute-done((bf16[2,128,8,128]{3,2,1,0:T(8,128)(2,1)}, bf16[2,128,8,128]{3,2,1,0:T(8,128)(2,1)}, u32[]{:S(2)}, u32[]{:S(2)}) %collective-permute-start.1) | collective-permute-done | bytes 524320 | tf_op jit(solution)/shard_map/ppermute | solution.py:23
  97.6 2.9 %collective-permute-done.2 = bf16[2,128,8,128]{3,2,1,0:T(8,128)(2,1)} collective-permute-done((bf16[2,128,8,128]{3,2,1,0:T(8,128)(2,1)}, bf16[2,128,8,128]{3,2,1,0:T(8,128)(2,1)}, u32[]{:S(2)}, u32[]{:S(2)}) %collective-permute-start.2) | collective-permute-done | bytes 524320 | tf_op jit(solution)/shard_map/ppermute | solution.py:23
  100.5 1.6 fusion.21
  105.4 165.8 %project.1 = (bf16[8,128,672]{2,1,0:T(8,128)(2,1)}, f32[1024,672]{1,0:T(8,128)}, f32[8,128]{1,0:T(8,128)}) custom-call(bf16[128,4096]{1,0:T(8,128)(2,1)} %pad_maximum_fusion.refs_0_, bf16[672,4096]{1,0:T(8,128)(2,1)} %refs_1_.1, bf16[8,128,672]{2,1,0:T(8,128)(2,1)} %get-tuple-element.10.refs_2_, f32[8,128]{1,0:T(8,128)} %select_maximum_fusion.refs_3_), custom_call_target="tpu_custom_call" | custom-call | tf_op jit(solution)/shard_map/project/pallas_call | solution.py:289
  271.2 1.9 copy.99
  273.1 1.5 copy.100
  274.7 3.4 %copy.101 = f32[1024,672]{0,1:T(8,128)} copy(f32[1024,672]{1,0:T(8,128)} %get-tuple-element.27) | data formatting | bytes 5505024
  278.1 1.3 slice_bitcast_fusion.3
  (82 shorter events, 19.3 us)
Async XLA Ops:
  1.7 5.6 %copy-start.11 = (f32[128]{0:T(128)S(1)}, f32[128]{0:T(128)}, u32[]{:S(2)}) copy-start(f32[128]{0:T(128)} %param.18) | copy-start | bytes 1540
  42.3 2.1 copy-start.8
  43.7 1.6 copy-start.10
  45.7 6.6 %copy-start.12 = (s32[1,128]{1,0:T(1,128)S(1)}, s32[1,128]{1,0:T(1,128)}, u32[]{:S(2)}) copy-start(s32[1,128]{1,0:T(1,128)} %param.15) | copy-start | bytes 1540
  52.3 3.1 %copy-start.9 = (bf16[128,8,2,128,1]{0,3,2,4,1:T(8,128)(2,1)S(1)}, bf16[128,8,2,128,1]{0,3,2,4,1:T(8,128)(2,1)}, u32[]{:S(2)}) copy-start(bf16[128,8,2,128,1]{0,3,2,4,1:T(8,128)(2,1)} %copy.113) | copy-start | bytes 1572868
  55.4 2.4 copy-start.7
  59.2 2.7 copy-start.5
  60.6 1.3 copy-start
  67.2 3.4 %copy-start.3 = (f32[8,4,128,128]{3,2,1,0:T(8,128)S(1)}, f32[8,4,128,128]{3,2,1,0:T(8,128)}, u32[]{:S(2)}) copy-start(f32[8,4,128,128]{3,2,1,0:T(8,128)} %fusion.10) | copy-start | bytes 6291460
  70.6 7.8 %copy-start.1 = (bf16[8,2,128,4,128]{2,4,1,3,0:T(8,128)(2,1)S(1)}, bf16[8,2,128,4,128]{2,4,1,3,0:T(8,128)(2,1)}, u32[]{:S(2)}) copy-start(bf16[8,2,128,4,128]{2,4,1,3,0:T(8,128)(2,1)} %copy-done) | copy-start | bytes 6291460
  72.8 17.5 %collective-permute-start = (bf16[2,128,8,128]{3,2,1,0:T(8,128)(2,1)}, bf16[2,128,8,128]{3,2,1,0:T(8,128)(2,1)}, u32[]{:S(2)}, u32[]{:S(2)}) collective-permute-start(bf16[2,128,8,128]{3,2,1,0:T(8,128)(2,1)} %pad_maximum_fusion.2), channel_id=1, source_target_pairs={{1,0},{2,1},{3,2},{5,4},{6,5},{7,6},{9,8},{10,9},{11,10},{13,12},{... | collective-permute-start | bytes 1572872 | tf_op jit(solution)/shard_map/ppermute | solution.py:23
  74.9 22.7 %collective-permute-start.1 = (bf16[2,128,8,128]{3,2,1,0:T(8,128)(2,1)}, bf16[2,128,8,128]{3,2,1,0:T(8,128)(2,1)}, u32[]{:S(2)}, u32[]{:S(2)}) collective-permute-start(bf16[2,128,8,128]{3,2,1,0:T(8,128)(2,1)} %pad_maximum_fusion.3), channel_id=1, source_target_pairs={{2,0},{3,1},{6,4},{7,5},{10,8},{11,9},{14,12},{15,13},{18,16},{19,... | collective-permute-start | bytes 1572872 | tf_op jit(solution)/shard_map/ppermute | solution.py:23
  77.1 23.4 %collective-permute-start.2 = (bf16[2,128,8,128]{3,2,1,0:T(8,128)(2,1)}, bf16[2,128,8,128]{3,2,1,0:T(8,128)(2,1)}, u32[]{:S(2)}, u32[]{:S(2)}) collective-permute-start(bf16[2,128,8,128]{3,2,1,0:T(8,128)(2,1)} %pad_maximum_fusion.4), channel_id=1, source_target_pairs={{3,0},{7,4},{11,8},{15,12},{19,16},{23,20},{27,24},{31,28}} | collective-permute-start | bytes 1572872 | tf_op jit(solution)/shard_map/ppermute | solution.py:23
  81.8 2.9 %copy-start.4 = (f32[8,4,128,128]{3,2,1,0:T(8,128)S(1)}, f32[8,4,128,128]{3,2,1,0:T(8,128)}, u32[]{:S(2)}) copy-start(f32[8,4,128,128]{3,2,1,0:T(8,128)} %fusion.10) | copy-start | bytes 6291460
  83.7 2.2 copy-start.2
  88.0 12.5 %copy-start.6 = (f32[1,128,8,128]{3,2,1,0:T(8,128)S(1)}, f32[1,128,8,128]{3,2,1,0:T(8,128)}, u32[]{:S(2)}) copy-start(f32[1,128,8,128]{3,2,1,0:T(8,128)} %slice.86) | copy-start | bytes 1572868
